TPU v7x, 512 devices: a whole 4x8x8 slice. The times are simulated.
512 devices in a mesh: rows: 64 (over z, y_hi, core), chan: 8 (over y_lo, x).
Axes of the slice: x: 4, y: 8 (y_hi: 4, y_lo: 2; y = y_hi * 2 + y_lo), z: 8, core: 2. Of those that a mesh axis runs over, the one named last changes fastest.
Arguments:
- pair: bfloat16 [512, 512, 128], P('rows', 'chan'), may hold values from -6 to 6
- block_mask: int32 [4, 4], replicated, may hold values from 0 to 1, as said below
- w_in: bfloat16 [128, 640], replicated, may hold values from -0.5 to 0.5
- w_out: bfloat16 [128, 128], replicated, may hold values from -0.5 to 0.5
Outputs:
- update: bfloat16 [512, 512, 128], P('rows', 'chan')
Inputs may be any that keep to these rules, and one draw needn't show every extreme that they name: Every diagonal entry of block_mask is 1; other entries are 0 or 1.
All inputs are finite; a program needn't handle non-finite values.
Results may differ from a plain program's by a relative error of at most 0.0078.
Values may be sent and summed in bfloat16 or wider, within the bound.
A program may use at most 64 MiB of HBM per device.

v0:
```python
import jax
import jax.numpy as jnp
from jax import lax
from jax.sharding import PartitionSpec as P

BLOCK = 128


def layer_norm(values):
    mean = jnp.mean(values, axis=-1, keepdims=True)
    centered = values - mean
    var = jnp.mean(centered * centered, axis=-1, keepdims=True)
    return centered / jnp.sqrt(var + 1e-05)


def channel_product(left, piece):
    return jnp.einsum("cik,cjk->cij", left, piece, preferred_element_type=jnp.float32)


def on_device(pair, block_mask, w_in, w_out):
    rows_dev, cols_dev, width = pair.shape
    n_blocks = block_mask.shape[0]
    row_start = lax.axis_index("rows") * rows_dev
    col_start = lax.axis_index("chan") * cols_dev
    row_ids = row_start + lax.broadcasted_iota(jnp.int32, (rows_dev, n_blocks), 0)
    col_ids = col_start + lax.broadcasted_iota(jnp.int32, (cols_dev, n_blocks), 0)
    rows_hot = (
        row_ids // BLOCK == lax.broadcasted_iota(jnp.int32, (rows_dev, n_blocks), 1)
    ).astype(jnp.float32)
    cols_hot = (
        col_ids // BLOCK == lax.broadcasted_iota(jnp.int32, (cols_dev, n_blocks), 1)
    ).astype(jnp.float32)
    mask_float = block_mask.astype(jnp.float32)
    local_mask = jnp.dot(jnp.dot(rows_hot, mask_float), cols_hot.T)[:, :, None]
    normed = layer_norm(pair.astype(jnp.float32)).astype(jnp.bfloat16)
    proj = jnp.dot(normed.reshape(-1, width), w_in, preferred_element_type=jnp.float32).reshape(
        rows_dev, cols_dev, 5 * width
    )
    left = (jax.nn.sigmoid(proj[..., :width]) * proj[..., width : 2 * width] * local_mask).astype(
        jnp.bfloat16
    )
    right = (
        jax.nn.sigmoid(proj[..., 2 * width : 3 * width])
        * proj[..., 3 * width : 4 * width]
        * local_mask
    ).astype(jnp.bfloat16)
    gate = jax.nn.sigmoid(proj[..., 4 * width :])
    left_t = jnp.transpose(left, (2, 0, 1))
    right_t = jnp.transpose(right, (2, 0, 1))
    left_ch, right_ch = (
        lax.all_to_all(left_t, "chan", split_axis=0, concat_axis=2, tiled=True),
        lax.all_to_all(right_t, "chan", split_axis=0, concat_axis=2, tiled=True),
    )
    prod_ch = channel_product(left_ch, lax.all_gather(right_ch, "rows", axis=1, tiled=True))
    prod_back = lax.all_to_all(prod_ch, "chan", split_axis=2, concat_axis=0, tiled=True)
    prod = jnp.transpose(prod_back, (1, 2, 0))
    normed_prod = layer_norm(prod).astype(jnp.bfloat16)
    mixed = jnp.dot(
        normed_prod.reshape(-1, width), w_out, preferred_element_type=jnp.float32
    ).reshape(rows_dev, cols_dev, width)
    return (gate * mixed).astype(jnp.bfloat16)


def solution(mesh):
    placed = (P("rows", "chan", None), P(), P(), P())
    return jax.shard_map(
        on_device, mesh=mesh, in_specs=placed, out_specs=P("rows", "chan", None), check_vma=False
    )
```

profile of v0, /device:TPU:16, one launch (start us, length us, event | category | flops | bytes accessed | tf_op | source)
XLA Modules:
  0.0 163.1 jit_solution(1687024607968159567)
XLA Ops:
  6.6 1.1 convert_reduce_fusion
  7.7 1.2 fusion.6
  8.9 1.3 fusion.22
  10.2 1.1 fusion.1
  11.3 0.2 fusion.28
  11.5 0.2 copy.23
  11.7 0.2 reshape.37
  11.9 11.7 %all_to_all.54 = bf16[8,2,4096]{2,1,0:T(2,128)(2,1)S(1)} all-to-all(bf16[8,2,4096]{2,1,0:T(2,128)(2,1)S(1)} %reshape.37), channel_id=1, replica_groups=mesh['rows'=64,'chan'=8] {'chan'}, dimensions={0} | all-to-all | bytes 262144 | tf_op jit(solution)/shard_map/all_to_all | solution.py:52
  23.6 0.2 reshape.38
  23.8 0.2 copy.24
  24.0 0.9 all_to_all.46
  24.9 0.0 all-gather.2.cloned.1.call-update
  24.9 0.2 copy.21
  25.1 0.2 reshape.35
  25.4 9.1 %all_to_all.55 = bf16[8,2,4096]{2,1,0:T(2,128)(2,1)S(1)} all-to-all(bf16[8,2,4096]{2,1,0:T(2,128)(2,1)S(1)} %reshape.35), channel_id=1, replica_groups=mesh['rows'=64,'chan'=8] {'chan'}, dimensions={0} | all-to-all | bytes 262144 | tf_op jit(solution)/shard_map/all_to_all | solution.py:51
  34.5 0.2 reshape.36
  34.7 0.2 copy.22
  34.9 0.2 all_to_all.42
  35.1 93.4 %all-gather.2.cloned.1.call-done = bf16[16,512,512]{2,1,0:T(8,128)(2,1)} async-done(((bf16[16,8,512]{2,1,0:T(8,128)(2,1)}), bf16[16,512,512]{2,1,0:T(8,128)(2,1)}) %all-gather.2.cloned.1.call-update) | async-done | bytes 8388624 | tf_op jit(solution)/shard_map/all_gather | solution.py:54
  128.4 5.6 %fusion.41 = f32[16,8,512]{2,1,0:T(8,128)S(1)} fusion(bf16[16,8,512]{2,1,0:T(8,128)(2,1)S(1)} %all_to_all.42, bf16[16,512,512]{2,1,0:T(8,128)(2,1)} %all-gather.2.cloned.1.call-done), kind=kOutput, calls=%fused_computation.65 | convolution fusion | flops 67108864 | bytes 8781824 | tf_op jit(solution)/shard_map/cik,cjk->cij/dot_general | solution.py:17
  134.1 0.8 copy.25
  134.9 0.7 reshape.39
  135.7 15.2 %all_to_all.56 = f32[8,1,8192]{2,1,0:T(1,128)S(1)} all-to-all(f32[8,1,8192]{2,1,0:T(1,128)S(1)} %reshape.39), channel_id=1, replica_groups=mesh['rows'=64,'chan'=8] {'chan'}, dimensions={0} | all-to-all | bytes 524288 | tf_op jit(solution)/shard_map/all_to_all | solution.py:55
  150.9 0.5 broadcast.132
  151.4 1.3 reduce
  152.7 0.7 reshape.40
  153.4 0.0 copy-start.2
  153.4 0.6 copy.26
  154.1 0.1 bitcast_reduce_fusion
  154.2 0.1 multiply_reduce_fusion
  154.4 0.1 divide_convert_fusion
  154.4 1.8 %fusion = bf16[8,64,128]{2,1,0:T(8,128)(2,1)} fusion(f32[8,64,640]{2,1,0:T(8,128)} %copy-done.1, bf16[8,64,128]{1,0,2:T(8,128)(2,1)S(1)} %divide_convert_fusion, bf16[128,128]{1,0:T(8,128)(2,1)S(1)} %copy-done.2), kind=kOutput, calls=%fused_computation.1 | convolution fusion | flops 17104896 | bytes 557056 | tf_op jit(solution)/shard_map/dot_general | solution.py:58
  (14 shorter events, 0.1 us)
Async XLA Ops:
  6.5 2.4 %copy-start = (bf16[128,640]{1,0:T(8,128)(2,1)S(1)}, bf16[128,640]{1,0:T(8,128)(2,1)}, u32[]{:S(2)}) copy-start(bf16[128,640]{1,0:T(8,128)(2,1)} %param.6) | copy-start | bytes 491524
  6.5 121.9 %all-gather.2.cloned.1.call-start = ((), (), s32[]{:S(2)}) async-start(), calls=%async_computation.3 | async-start | bytes 8519680 | tf_op jit(solution)/shard_map/all_gather | solution.py:54
  10.2 14.7 %copy-start.1 = (f32[8,64,640]{2,1,0:T(8,128)}, f32[8,64,640]{2,1,0:T(8,128)S(1)}, u32[]{:S(2)}) copy-start(f32[8,64,640]{2,1,0:T(8,128)S(1)} %fusion.22) | copy-start | bytes 3932164
  153.4 1.0 copy-start.2
Sparse Core Ops, SparseCore 0:
  25.0 103.3 all-gather.1
where the time goes:
time: 163 us
  waiting for transfers between devices  93.4 us (57%)
  blocking collectives  36 us (22%)
  between operations  13.6 us (8%)
  matrix products  9.88 us (6%)
  local copies, waits for them, and re-layouts  6.17 us (4%)
  other arithmetic  4.1 us (3%)
    all_gather x1, waiting for transfers between devices, on_device(): lax.all_gather(right_ch, 'rows', axis=1, tiled=True)  93.4 us
    all_to_all x1, blocking collectives, on_device(): lax.all_to_all(prod_ch, 'chan', split_axis=2, concat_axis=0, tiled=True)  15.2 us
    all_to_all x1, blocking collectives, on_device(): lax.all_to_all(right_t, 'chan', split_axis=0, concat_axis=2, tiled=True)  11.7 us
    all_to_all x1, blocking collectives, on_device(): lax.all_to_all(left_t, 'chan', split_axis=0, concat_axis=2, tiled=True)  9.11 us
    dot_general x1, matrix products, channel_product(): jnp.einsum('cik,cjk->cij', left, piece, preferred_element_type=jnp.float32)  5.63 us
  transfers between devices with their start and end apart: 1, of which 1 were waited for; matrix products, arithmetic and copies ran while one was open for 0% of the time, Pallas kernels for 0%

commit v1 on v0

--- a/solution.py
+++ b/solution.py
@@ -51,7 +51,12 @@
         lax.all_to_all(left_t, "chan", split_axis=0, concat_axis=2, tiled=True),
         lax.all_to_all(right_t, "chan", split_axis=0, concat_axis=2, tiled=True),
     )
-    prod_ch = channel_product(left_ch, lax.all_gather(right_ch, "rows", axis=1, tiled=True))
+    prod_ch = channel_product(
+        left_ch,
+        jnp.concatenate(
+            lax.all_to_all(jnp.stack([right_ch] * lax.axis_size("rows")), "rows", 0, 0), axis=1
+        ),
+    )
     prod_back = lax.all_to_all(prod_ch, "chan", split_axis=2, concat_axis=0, tiled=True)
     prod = jnp.transpose(prod_back, (1, 2, 0))
     normed_prod = layer_norm(prod).astype(jnp.bfloat16)

time: 163 us -> 301 us (1.85)
  the two profiles are of different devices: /device:TPU:16 before, /device:TPU:144 now
where the time goes in v1:
time: 301 us; the launch traced here: 300 us
  waiting for transfers between devices  221 us (73%)
  blocking collectives  31.2 us (10%)
  starting transfers between devices  22.6 us (8%)
  local copies, waits for them, and re-layouts  11 us (4%)
  matrix products  9.89 us (3%)
  other arithmetic  4.1 us (1%)
    all_to_all x1, waiting for transfers between devices, on_device(): lax.all_to_all(jnp.stack([right_ch] * lax.axis_size('rows')), 'rows', 0, 0)  210 us
    all_to_all x1, blocking collectives, on_device(): lax.all_to_all(prod_ch, 'chan', split_axis=2, concat_axis=0, tiled=True)  31.2 us
    all_to_all x1, starting transfers between devices, on_device(): lax.all_to_all(jnp.stack([right_ch] * lax.axis_size('rows')), 'rows', 0, 0)  13.9 us
  transfers between devices with their start and end apart: 3, of which 3 were waited for; matrix products, arithmetic and copies ran while one was open for 1% of the time, Pallas kernels for 0%

profile of v1, /device:TPU:144, one launch (start us, length us, event | category | flops | bytes accessed | tf_op | source)
XLA Modules:
  0.0 300.2 jit_solution(16976261848968433075)
XLA Ops:
  0.1 1.1 convert_reduce_fusion
  1.2 1.2 fusion.9
  2.4 1.3 fusion.25
  3.7 1.1 fusion.4
  4.8 0.2 fusion.31
  5.0 0.2 copy.23
  5.1 0.9 reshape.48
  6.0 5.3 %all-to-all-start.1 = ((bf16[8,2,4096]{2,1,0:T(2,128)(2,1)}), bf16[8,2,4096]{2,1,0:T(2,128)(2,1)S(1)}, u32[]{:S(2)}, u32[]{:S(2)}) async-start(bf16[8,2,4096]{2,1,0:T(2,128)(2,1)} %reshape.48), calls=%async_computation.1 | async-start | bytes 262144 | tf_op jit(solution)/shard_map/all_to_all | solution.py:52
  11.3 0.2 copy.21
  11.5 0.9 reshape.46
  12.4 5.5 %all-to-all-done.1 = bf16[8,2,4096]{2,1,0:T(2,128)(2,1)S(1)} async-done(((bf16[8,2,4096]{2,1,0:T(2,128)(2,1)}), bf16[8,2,4096]{2,1,0:T(2,128)(2,1)S(1)}, u32[]{:S(2)}, u32[]{:S(2)}) %all-to-all-start.1) | async-done | bytes 131104 | tf_op jit(solution)/shard_map/all_to_all | solution.py:52
  17.9 3.4 %all-to-all-start = ((bf16[8,2,4096]{2,1,0:T(2,128)(2,1)}), bf16[8,2,4096]{2,1,0:T(2,128)(2,1)S(1)}, u32[]{:S(2)}, u32[]{:S(2)}) async-start(bf16[8,2,4096]{2,1,0:T(2,128)(2,1)} %reshape.46), calls=%async_computation | async-start | bytes 262144 | tf_op jit(solution)/shard_map/all_to_all | solution.py:51
  21.3 0.2 reshape.49
  21.5 0.2 copy.24
  21.7 0.2 stack.4
  21.9 5.9 %all-to-all-done = bf16[8,2,4096]{2,1,0:T(2,128)(2,1)S(1)} async-done(((bf16[8,2,4096]{2,1,0:T(2,128)(2,1)}), bf16[8,2,4096]{2,1,0:T(2,128)(2,1)S(1)}, u32[]{:S(2)}, u32[]{:S(2)}) %all-to-all-start) | async-done | bytes 131104 | tf_op jit(solution)/shard_map/all_to_all | solution.py:51
  27.8 4.2 %stack.5 = bf16[64,16,8,512]{3,2,1,0:T(8,128)(2,1)} broadcast(bf16[16,8,512]{2,1,0:T(8,128)(2,1)S(1)} %stack.4), dimensions={1,2,3} | broadcast | bytes 8519680 | tf_op jit(solution)/shard_map/stack | solution.py:57
  32.0 13.9 %all-to-all-start.2 = ((bf16[64,16,8,512]{3,2,1,0:T(8,128)(2,1)}), bf16[64,16,8,512]{3,2,1,0:T(8,128)(2,1)}, u32[]{:S(2)}, u32[]{:S(2)}) async-start(bf16[64,16,8,512]{3,2,1,0:T(8,128)(2,1)} %stack.5), calls=%async_computation.2 | async-start | bytes 16777216 | tf_op jit(solution)/shard_map/all_to_all | solution.py:57
  46.0 0.2 reshape.47
  46.2 0.2 copy.22
  46.4 0.2 all_to_all.43
  46.6 209.7 %all-to-all-done.2 = bf16[64,16,8,512]{3,2,1,0:T(8,128)(2,1)} async-done(((bf16[64,16,8,512]{3,2,1,0:T(8,128)(2,1)}), bf16[64,16,8,512]{3,2,1,0:T(8,128)(2,1)}, u32[]{:S(2)}, u32[]{:S(2)}) %all-to-all-start.2) | async-done | bytes 8388640 | tf_op jit(solution)/shard_map/all_to_all | solution.py:57
  256.3 5.6 %fusion = f32[16,8,512]{2,1,0:T(8,128)S(1)} fusion(bf16[16,8,512]{2,1,0:T(8,128)(2,1)S(1)} %all_to_all.43, bf16[64,16,8,512]{3,2,1,0:T(8,128)(2,1)} %all-to-all-done.2), kind=kOutput, calls=%fused_computation | convolution fusion | flops 67108864 | bytes 8781824 | tf_op jit(solution)/shard_map/cik,cjk->cij/dot_general | solution.py:17
  262.0 0.8 copy.26
  262.8 0.7 reshape.50
  263.6 31.2 %all_to_all.56 = f32[8,1,8192]{2,1,0:T(1,128)S(1)} all-to-all(f32[8,1,8192]{2,1,0:T(1,128)S(1)} %reshape.50), channel_id=1, replica_groups=mesh['rows'=64,'chan'=8] {'chan'}, dimensions={0} | all-to-all | bytes 524288 | tf_op jit(solution)/shard_map/all_to_all | solution.py:60
  294.8 0.5 broadcast.133
  295.3 1.3 reduce
  296.6 0.7 reshape.51
  297.3 0.6 copy.27
  297.9 0.1 bitcast_reduce_fusion
  298.3 1.8 fusion.3
  (16 shorter events, 0.3 us)
Async XLA Ops:
  0.0 2.3 copy-start
  3.7 28.4 %copy-start.1 = (f32[8,64,640]{2,1,0:T(8,128)}, f32[8,64,640]{2,1,0:T(8,128)S(1)}, u32[]{:S(2)}) copy-start(f32[8,64,640]{2,1,0:T(8,128)S(1)} %fusion.25) | copy-start | bytes 3932164
  6.0 11.9 %all-to-all-start.1 = ((bf16[8,2,4096]{2,1,0:T(2,128)(2,1)}), bf16[8,2,4096]{2,1,0:T(2,128)(2,1)S(1)}, u32[]{:S(2)}, u32[]{:S(2)}) async-start(bf16[8,2,4096]{2,1,0:T(2,128)(2,1)} %reshape.48), calls=%async_computation.1 | async-start | bytes 262144 | tf_op jit(solution)/shard_map/all_to_all | solution.py:52
  17.9 9.9 %all-to-all-start = ((bf16[8,2,4096]{2,1,0:T(2,128)(2,1)}), bf16[8,2,4096]{2,1,0:T(2,128)(2,1)S(1)}, u32[]{:S(2)}, u32[]{:S(2)}) async-start(bf16[8,2,4096]{2,1,0:T(2,128)(2,1)} %reshape.46), calls=%async_computation | async-start | bytes 262144 | tf_op jit(solution)/shard_map/all_to_all | solution.py:51
  32.0 224.3 %all-to-all-start.2 = ((bf16[64,16,8,512]{3,2,1,0:T(8,128)(2,1)}), bf16[64,16,8,512]{3,2,1,0:T(8,128)(2,1)}, u32[]{:S(2)}, u32[]{:S(2)}) async-start(bf16[64,16,8,512]{3,2,1,0:T(8,128)(2,1)} %stack.5), calls=%async_computation.2 | async-start | bytes 16777216 | tf_op jit(solution)/shard_map/all_to_all | solution.py:57
  262.0 36.3 %copy-start.2 = (bf16[128,128]{1,0:T(8,128)(2,1)S(1)}, bf16[128,128]{1,0:T(8,128)(2,1)}, u32[]{:S(2)}) copy-start(bf16[128,128]{1,0:T(8,128)(2,1)} %param.7) | copy-start | bytes 98308
